TPU v7x, 128 devices: a whole 4x4x4 slice. The times are simulated.
128 devices in a mesh: seq: 8 (over x, core), exp: 16 (over y, z).
Axes of the slice: x: 4, y: 4, z: 4, core: 2. Of those that a mesh axis runs over, the one named last changes fastest.
Arguments:
- xin: bfloat16 [512, 4, 8192], P('seq', None, 'exp'), may hold values from -6 to 6
- zin: bfloat16 [512, 4, 8192], P('seq', None, 'exp'), may hold values from -6 to 6
- conv_weight: float32 [4, 8192], P(None, 'exp'), may hold values from -3 to 3
- conv_bias: float32 [8192], P('exp'), may hold values from -3 to 3
- xproj_weight: bfloat16 [8192, 288], P('exp'), may hold values from -0.0625 to 0.0625
- dtproj_weight: bfloat16 [256, 8192], P(None, 'exp'), may hold values from -0.375 to 0.375
- dt_bias: float32 [8192], P('exp'), may hold values from -5 to -3
- a_log: float32 [16, 8192], P(None, 'exp'), may hold values from -3 to 1
- skip: float32 [8192], P('exp'), may hold values from 0.2 to 1
- out_weight: bfloat16 [8192, 4096], P('exp'), may hold values from -0.0625 to 0.0625
- resid: bfloat16 [512, 4, 4096], P(('seq', 'exp')), may hold values from -6 to 6
- norm_gain: float32 [4096], replicated, may hold values from 0.5 to 1.5
- expert_ids: int32 [512, 4, 2], P(('seq', 'exp')), may hold values from 0 to 7, all different within a row; in each aligned block of 16 rows (0 to 15, 16 to 31, ..., all dimensions but the last counted through in order) at most 8 rows name the same one
- gate_weights: bfloat16 [512, 4, 2], P(('seq', 'exp')), may hold values from 0.19921875 to 1
- w_gate: bfloat16 [16, 4096, 6144], P('exp', None, 'seq'), may hold values from -0.09375 to 0.09375
- w_up: bfloat16 [16, 4096, 6144], P('exp', None, 'seq'), may hold values from -0.09375 to 0.09375
- w_down: bfloat16 [16, 6144, 4096], P('exp', 'seq'), may hold values from -0.0546875 to 0.0546875
Outputs:
- layer_out: bfloat16 [512, 4, 4096], P(('seq', 'exp'))
Inputs may be any that keep to these rules, and one draw needn't show every extreme that they name: `expert_ids`: tokens are ordered by position, then document; in each aligned block of 16 such tokens (the tokens of one device), every expert is named at most 8 times, and in every draw some expert is named exactly 8 times in some block. Each token names 2 different experts.
All inputs are finite; a program needn't handle non-finite values.
Results may differ from a plain program's by a relative error of at most 0.03.
Values may be sent and summed in bfloat16 or wider, within the bound.
No kernel may reach another device: no remote copies, remote signals or barrier semaphores. Data moves between devices by JAX's collectives and lax.ppermute only.
A program may use at most 128 MiB of HBM per device.

v0:
```python
import jax
import jax.numpy as jnp
from jax import lax
from jax.sharding import PartitionSpec as P

D = 4096
STATE = 16
CONV = 4
RANK = 256
EXPERTS = 8
TOPK = 2


def passed_along(value, axis, by):
    count = lax.axis_size(axis)
    pairs = [(i, i + by) for i in range(count) if 0 <= i + by < count]
    return lax.ppermute(value, axis, pairs)


def entering(value, axis, join, neutral):
    place = lax.axis_index(axis)
    gathered = jax.tree.map(
        lambda a, kind: lax.all_gather(a.astype(kind), axis), value, (jnp.bfloat16, jnp.bfloat16)
    )
    state = jax.tree.map(lambda a, e: jnp.zeros_like(a) + jnp.asarray(e, a.dtype), value, neutral)

    def one(step, state):
        return join(
            state,
            jax.tree.map(
                lambda a, own: lax.dynamic_index_in_dim(a, step, 0, False).astype(own.dtype),
                gathered,
                value,
            ),
        )

    return lax.fori_loop(0, place, one, state)


def conv_inputs(window, conv_weight, conv_bias, length):
    running = jnp.zeros(window[:length].shape, jnp.float32) + conv_bias
    for offset in range(CONV):
        running = running + conv_weight[offset] * window[offset : offset + length]
    return running


def make_step(decay_rate):

    def advance(carry_state, series_now):
        step_now, input_now, read_now, value_now = series_now
        factor = jnp.exp(step_now[:, None, :] * decay_rate[None])
        carry_state = (
            factor * carry_state + (step_now * value_now)[:, None, :] * input_now[:, :, None]
        )
        return (carry_state, jnp.sum(read_now[:, :, None] * carry_state, axis=1))

    return advance


def chain(earlier, later):
    return (earlier[0] * later[0], later[0] * earlier[1] + later[1])


def slot_select(route_ids, capacity):
    flat_ids = route_ids.reshape(-1)
    onehot = (flat_ids[:, None] == jnp.arange(EXPERTS, dtype=jnp.int32)[None, :]).astype(jnp.int32)
    before = jnp.sum((jnp.cumsum(onehot, axis=0) - onehot) * onehot, axis=1)
    target = flat_ids * capacity + before
    matches = jnp.arange(EXPERTS * capacity, dtype=jnp.int32)[:, None] == target[None, :]
    return matches.reshape(EXPERTS * capacity, route_ids.shape[0], route_ids.shape[1])


def per_device(
    xin,
    zin,
    conv_weight,
    conv_bias,
    xproj_weight,
    dtproj_weight,
    dt_bias,
    a_log,
    skip,
    out_weight,
    resid,
    norm_gain,
    expert_ids,
    gate_weights,
    w_gate,
    w_up,
    w_down,
):
    section = xin.shape[0]
    edge_rows = passed_along(xin[section - (CONV - 1) :], "seq", 1)
    window = jnp.concatenate([edge_rows, xin], axis=0).astype(jnp.float32)
    inner_act = jax.nn.silu(conv_inputs(window, conv_weight, conv_bias, section)).astype(
        jnp.bfloat16
    )
    inner_f = inner_act.astype(jnp.float32)
    projected = jnp.einsum(
        "pbc,cr->pbr", inner_act, xproj_weight, preferred_element_type=jnp.float32
    )
    projected = lax.psum(projected.astype(jnp.bfloat16), "exp").astype(jnp.float32)
    low_rank = projected[..., :RANK].astype(jnp.bfloat16)
    in_state = projected[..., RANK : RANK + STATE]
    out_state = projected[..., RANK + STATE :]
    step_size = jax.nn.softplus(
        jnp.einsum("pbr,rc->pbc", low_rank, dtproj_weight, preferred_element_type=jnp.float32)
        + dt_bias
    )
    decay_rate = -jnp.exp(a_log)
    advance = make_step(decay_rate)
    series = (step_size, in_state, out_state, inner_f)
    zero_state = jnp.zeros((xin.shape[1], STATE, xin.shape[2]), jnp.float32)
    final_local, local_out = lax.scan(advance, zero_state, series)
    total_decay = jnp.exp(jnp.sum(step_size, axis=0)[:, None, :] * decay_rate[None])
    identity = (jnp.ones_like(total_decay), jnp.zeros_like(final_local))
    incoming = entering((total_decay, final_local), "seq", chain, identity)[1]
    ignored, ssm_out = lax.scan(advance, incoming, series)
    mixed_in = ((ssm_out + skip * inner_f) * jax.nn.silu(zin.astype(jnp.float32))).astype(
        jnp.bfloat16
    )
    row_block = mixed_in
    mamba_rows = lax.psum_scatter(
        jnp.einsum("pbc,cd->pbd", row_block, out_weight, preferred_element_type=jnp.float32).astype(
            jnp.bfloat16
        ),
        "exp",
        scatter_dimension=0,
        tiled=True,
    ).astype(jnp.float32)
    hidden_state = resid.astype(jnp.float32) + mamba_rows
    norm_scale = lax.rsqrt(jnp.mean(hidden_state * hidden_state, axis=-1, keepdims=True) + 1e-05)
    normed = (hidden_state * norm_scale * norm_gain).astype(jnp.bfloat16)
    row_count = resid.shape[0] * resid.shape[1]
    capacity = 2 * TOPK * row_count // EXPERTS
    splits = lax.axis_size("exp") // EXPERTS
    tokens = normed.reshape(row_count, D)
    route_ids = expert_ids.reshape(row_count, TOPK)
    gate_vals = gate_weights.reshape(row_count, TOPK)
    matches = slot_select(route_ids, capacity)
    chosen = jnp.sum(matches.astype(jnp.int32), axis=2).astype(jnp.bfloat16)
    outgoing = (
        jnp.dot(chosen, tokens, preferred_element_type=jnp.float32)
        .astype(jnp.bfloat16)
        .reshape(EXPERTS, capacity, D)
    )
    arrived = lax.all_to_all(
        jnp.tile(outgoing, (splits, 1, 1)), "exp", split_axis=0, concat_axis=0, tiled=True
    )
    everything = lax.all_gather(arrived, "seq", axis=0, tiled=True)
    row_block = everything
    expert_row_block = row_block.reshape(-1, D)
    gate_act = jnp.dot(expert_row_block, w_gate[0], preferred_element_type=jnp.float32)
    up_act = jnp.dot(expert_row_block, w_up[0], preferred_element_type=jnp.float32)
    hidden = (jax.nn.silu(gate_act) * up_act).astype(jnp.bfloat16)
    own_rows = lax.psum_scatter(
        jnp.dot(hidden, w_down[0], preferred_element_type=jnp.float32)
        .reshape(lax.axis_size("seq") * arrived.shape[0], capacity, D)
        .astype(jnp.bfloat16),
        "seq",
        scatter_dimension=0,
        tiled=True,
    ).astype(jnp.float32)
    returned = lax.all_to_all(
        own_rows.astype(jnp.bfloat16), "exp", split_axis=0, concat_axis=0, tiled=True
    ).astype(own_rows.dtype)
    summed = jnp.sum(returned.reshape(splits, EXPERTS * capacity, D), axis=0)
    weights = jnp.sum(matches.astype(jnp.float32) * gate_vals.astype(jnp.float32)[None], axis=2)
    expert_out = jnp.dot(weights.T, summed, precision=lax.Precision.HIGHEST)
    return (hidden_state + expert_out.reshape(hidden_state.shape)).astype(jnp.bfloat16)


def solution(mesh):
    placed = (
        P("seq", None, "exp"),
        P("seq", None, "exp"),
        P(None, "exp"),
        P("exp"),
        P("exp", None),
        P(None, "exp"),
        P("exp"),
        P(None, "exp"),
        P("exp"),
        P("exp", None),
        P(("seq", "exp"), None, None),
        P(),
        P(("seq", "exp"), None, None),
        P(("seq", "exp"), None, None),
        P("exp", None, "seq"),
        P("exp", None, "seq"),
        P("exp", "seq", None),
    )
    return jax.shard_map(
        per_device,
        mesh=mesh,
        in_specs=placed,
        out_specs=P(("seq", "exp"), None, None),
        check_vma=False,
    )
```

profile of v0, /device:TPU:2, one launch (start us, length us, event | category | flops | bytes accessed | tf_op | source)
XLA Modules:
  0.0 485.4 jit_solution(7767882943626385610)
XLA Ops:
  6.6 0.8 slice.38
  7.4 1.9 collective-permute-start
  9.3 0.9 fusion.43
  10.2 2.2 collective-permute-done
  12.4 1.1 maximum_convert_fusion
  13.5 1.2 fusion.39
  14.7 1.0 convolution_convert_fusion.3
  15.8 86.0 %all-reduce.4.cloned.1.call-done = bf16[64,4,288]{2,0,1:T(8,128)(2,1)} async-done(((bf16[64,4,288]{2,0,1:T(8,128)(2,1)}), bf16[64,4,288]{2,0,1:T(8,128)(2,1)}) %all-reduce.4.cloned.1.call-update) | async-done | bytes 147472 | tf_op jit(solution)/shard_map/psum | solution.py:102
  101.8 1.2 fusion.35
  103.6 1.7 fusion.42
  105.4 10.3 %while.37 = (s32[]{:T(128)}, f32[4,16,512]{2,1,0:T(8,128)S(1)}, f32[64,4,512]{2,1,0:T(4,128)S(1)}, f32[16,512]{1,0:T(8,128)S(1)}, f32[64,4,512]{2,1,0:T(4,128)S(...) while((s32[]{:T(128)}, f32[4,16,512]{2,1,0:T(8,128)S(1)}, f32[64,4,512]{2,1,0:T(4,128)S(1)}, ...), condition=%wide.region_3.4_spmd.clone, body=%wide.region_2.3_spmd.clone.sunk | while | flops 165891 | bytes 353131 | solution.py:114
  115.7 13.1 %all-gather = bf16[32,16,512]{2,1,0:T(8,128)(2,1)S(1)} all-gather(bf16[4,16,512]{2,1,0:T(8,128)(2,1)S(1)} %convert_element_type.103), channel_id=2, replica_groups=mesh['seq'=8,'exp'=16] {'seq'}, dimensions={0}, use_global_device_ids=true | all-gather | bytes 589824 | tf_op jit(solution)/shard_map/all_gather | solution.py:23
  128.9 13.1 %all_gather.13 = bf16[8,4,16,512]{3,2,1,0:T(8,128)(2,1)S(1)} all-gather(bf16[1,4,16,512]{3,2,1,0:T(8,128)(2,1)S(1)} %exponential_convert_fusion), channel_id=1, replica_groups=mesh['seq'=8,'exp'=16] {'seq'}, dimensions={0}, use_global_device_ids=true | all-gather | bytes 589824 | tf_op jit(solution)/shard_map/all_gather | solution.py:23
  142.2 58.7 %while.36 = (s32[]{:T(128)}, f32[4,16,512]{2,1,0:T(8,128)S(1)}, f32[64,4,512]{2,1,0:T(4,128)S(1)}, f32[64,4,512]{2,1,0:T(4,128)S(1)}, f32[16,512]{1,0:T(8,128)S(...) while((s32[]{:T(128)}, f32[4,16,512]{2,1,0:T(8,128)S(1)}, ...), condition=%wide.region_8.9_spmd, body=%wide.region_6.8_spmd.sunk | while | flops 196610 | bytes 378481 | solution.py:118
  179.7 0.8 constant_dynamic-slice_fusion.3
  180.7 0.8 constant_dynamic-slice_fusion.3
  183.5 0.8 constant_dynamic-slice_fusion.3
  184.4 0.8 constant_dynamic-slice_fusion.3
  200.9 1.3 fusion.30
  202.3 4.8 convolution_convert_fusion.1
  209.3 87.8 %all-reduce.6.cloned.1.call-done = bf16[64,4,4096]{2,0,1:T(8,128)(2,1)} async-done(((bf16[64,4,4096]{2,0,1:T(8,128)(2,1)}), bf16[64,4,4096]{2,0,1:T(8,128)(2,1)}) %all-reduce.6.cloned.1.call-update) | async-done | bytes 2097168
  297.1 1.0 constant_dynamic-slice_fusion.1
  299.1 20.6 %all_to_all.10 = bf16[16,8,4096]{2,1,0:T(8,128)(2,1)} all-to-all(bf16[16,8,4096]{2,1,0:T(8,128)(2,1)S(1)} %bitcast.113), channel_id=1, replica_groups=mesh['seq'=8,'exp'=16] {'exp'}, dimensions={0} | all-to-all | bytes 2097152 | tf_op jit(solution)/shard_map/all_to_all | solution.py:147
  319.9 46.7 %all-gather.3.cloned.1.call-done = bf16[128,8,4096]{2,1,0:T(8,128)(2,1)} async-done(((bf16[16,8,4096]{2,1,0:T(8,128)(2,1)}), bf16[128,8,4096]{2,1,0:T(8,128)(2,1)}) %all-gather.3.cloned.1.call-update) | async-done | bytes 8388624 | tf_op jit(solution)/shard_map/all_gather | solution.py:150
  366.6 11.0 %fusion.1 = f32[1024,768]{1,0:T(8,128)S(1)} fusion(bf16[128,8,4096]{2,1,0:T(8,128)(2,1)} %all-gather.3.cloned.1.call-done, bf16[1,4096,768]{2,1,0:T(8,128)(2,1)} %param.38), kind=kOutput, calls=%fused_computation.14 | convolution fusion | flops 6442450944 | bytes 17825792 | tf_op jit(solution)/shard_map/dot_general | solution.py:154
  377.7 9.9 %fusion.16 = bf16[128,8,768]{2,1,0:T(8,128)(2,1)S(1)} fusion(f32[1024,768]{1,0:T(8,128)S(1)} %fusion.1, bf16[1,4096,768]{2,1,0:T(8,128)(2,1)} %param.37, bf16[128,8,4096]{2,1,0:T(8,128)(2,1)S(1)} %copy-done.9), kind=kOutput, calls=%fused_computation.31 | convolution fusion | flops 6447169536 | bytes 19398656 | tf_op jit(solution)/shard_map/dot_general | solution.py:153
  387.6 8.9 %convolution_convert_fusion = bf16[128,8,4096]{2,0,1:T(8,128)(2,1)} fusion(bf16[1,768,4096]{2,1,0:T(8,128)(2,1)S(1)} %bitcast.122, bf16[128,8,768]{2,1,0:T(8,128)(2,1)S(1)} %fusion.16), kind=kOutput, calls=%fused_computation.18 | convolution fusion | flops 6446645248 | bytes 16252928 | tf_op jit(solution)/shard_map/dot_general | solution.py:157
  396.5 51.1 %reduce-scatter.3.cloned.1.call-done = bf16[16,8,4096]{2,0,1:T(8,128)(2,1)} async-done(((bf16[128,8,4096]{2,0,1:T(8,128)(2,1)}), bf16[16,8,4096]{2,0,1:T(8,128)(2,1)}) %reduce-scatter.3.cloned.1.call-update) | async-done | bytes 1048592 | tf_op jit(solution)/shard_map/reduce_scatter | solution.py:156
  447.7 2.8 copy.87
  450.4 7.2 %all-to-all-start.1 = ((bf16[16,8,4096]{2,1,0:T(8,128)(2,1)}), bf16[16,8,4096]{2,1,0:T(8,128)(2,1)S(1)}, u32[]{:S(2)}, u32[]{:S(2)}) async-start(bf16[16,8,4096]{2,1,0:T(8,128)(2,1)} %copy.87), calls=%async_computation.2 | async-start | bytes 2097152 | tf_op jit(solution)/shard_map/all_to_all | solution.py:164
  457.9 19.5 %all-to-all-done.1 = bf16[16,8,4096]{2,1,0:T(8,128)(2,1)S(1)} async-done(((bf16[16,8,4096]{2,1,0:T(8,128)(2,1)}), bf16[16,8,4096]{2,1,0:T(8,128)(2,1)S(1)}, u32[]{:S(2)}, u32[]{:S(2)}) %all-to-all-start.1) | async-done | bytes 1048608 | tf_op jit(solution)/shard_map/all_to_all | solution.py:164
  477.5 1.4 fusion.9
  (706 shorter events, 65.0 us)
Async XLA Ops:
  6.5 8.1 %copy-start = (bf16[512,288]{0,1:T(8,128)(2,1)S(1)}, bf16[512,288]{0,1:T(8,128)(2,1)}, u32[]{:S(2)}) copy-start(bf16[512,288]{0,1:T(8,128)(2,1)} %param.27) | copy-start | bytes 884740
  6.5 9.2 %copy-start.3 = (f32[16,512]{1,0:T(8,128)S(1)}, f32[16,512]{1,0:T(8,128)}, u32[]{:S(2)}) copy-start(f32[16,512]{1,0:T(8,128)} %param.30) | copy-start | bytes 98308
  6.5 95.3 %copy-start.2 = (bf16[256,512]{1,0:T(8,128)(2,1)S(1)}, bf16[256,512]{1,0:T(8,128)(2,1)}, u32[]{:S(2)}) copy-start(bf16[256,512]{1,0:T(8,128)(2,1)} %param.28) | copy-start | bytes 786436
  6.5 95.3 %copy-start.6 = (f32[512]{0:T(512)S(1)}, f32[512]{0:T(512)}, u32[]{:S(2)}) copy-start(f32[512]{0:T(512)} %param.29) | copy-start | bytes 6148
  6.5 95.2 %all-reduce.4.cloned.1.call-start = ((), (), s32[]{:S(2)}) async-start(), calls=%async_computation.3 | async-start | bytes 393216 | tf_op jit(solution)/shard_map/psum | solution.py:102
  7.4 5.0 %collective-permute-start = (bf16[3,4,512]{2,1,0:T(4,128)(2,1)S(1)}, bf16[3,4,512]{2,1,0:T(4,128)(2,1)S(1)}, u32[]{:S(2)}, u32[]{:S(2)}) collective-permute-start(bf16[3,4,512]{2,1,0:T(4,128)(2,1)S(1)} %slice.38), channel_id=1, source_target_pairs={{0,16},{16,32},{32,48},{48,64},{64,80},{80,96},{96,112},{1,17},{17... | collective-permute-start | bytes 36872 | tf_op jit(solution)/shard_map/ppermute | solution.py:17
  15.7 281.4 %all-reduce.6.cloned.1.call-start = ((), (), s32[]{:S(2)}) async-start(), calls=%async_computation.6 | async-start | bytes 4194304
  105.3 95.6 %copy-start.7 = (f32[512]{0:T(512)S(1)}, f32[512]{0:T(512)}, u32[]{:S(2)}) copy-start(f32[512]{0:T(512)} %param.31) | copy-start | bytes 6148
  202.3 4.9 %copy-start.5 = (s32[4,4,2]{1,2,0:T(2,128)S(1)}, s32[4,4,2]{1,2,0:T(2,128)}, u32[]{:S(2)}) copy-start(s32[4,4,2]{1,2,0:T(2,128)} %param.35) | copy-start | bytes 388
  202.3 5.7 %copy-start.10 = (u32[128]{0:T(128)S(1)}, u32[128]{0:T(128)}, u32[]{:S(2)}) copy-start(u32[128]{0:T(128)} %constant.77) | copy-start | bytes 1540
  202.3 95.9 %copy-start.1 = (bf16[4,4,4096]{2,1,0:T(4,128)(2,1)S(1)}, bf16[4,4,4096]{2,1,0:T(4,128)(2,1)}, u32[]{:S(2)}) copy-start(bf16[4,4,4096]{2,1,0:T(4,128)(2,1)} %param.33) | copy-start | bytes 393220
  202.3 96.1 %copy-start.4 = (f32[4096]{0:T(1024)S(1)}, f32[4096]{0:T(1024)}, u32[]{:S(2)}) copy-start(f32[4096]{0:T(1024)} %param.34) | copy-start | bytes 49156
  207.1 159.5 %all-gather.3.cloned.1.call-start = ((), (), s32[]{:S(2)}) async-start(), calls=%async_computation.4 | async-start | bytes 9437184 | tf_op jit(solution)/shard_map/all_gather | solution.py:150
  319.7 128.0 %reduce-scatter.3.cloned.1.call-start = ((), (), s32[]{:S(2)}) async-start(), calls=%async_computation.5 | async-start | bytes 9437184 | tf_op jit(solution)/shard_map/reduce_scatter | solution.py:156
  366.6 11.0 %copy-start.9 = (bf16[128,8,4096]{2,1,0:T(8,128)(2,1)S(1)}, bf16[128,8,4096]{2,1,0:T(8,128)(2,1)}, u32[]{:S(2)}) copy-start(bf16[128,8,4096]{2,1,0:T(8,128)(2,1)} %all-gather.3.cloned.1.call-done) | copy-start | bytes 25165828
  366.6 21.0 %slice-start = ((s8[6291456]{0:T(1024)(128)(4,1)}), s8[4194304]{0:T(1024)(128)(4,1)S(1)}, s32[]{:S(2)}) async-start(s8[6291456]{0:T(1024)(128)(4,1)} %bitcast.121), calls=%async_computation.7 | async-start | bytes 8388608
  377.7 10.0 %slice-start.1 = ((s8[6291456]{0:T(1024)(128)(4,1)}), s8[2097152]{0:T(1024)(128)(4,1)S(1)}, s32[]{:S(2)}) async-start(s8[6291456]{0:T(1024)(128)(4,1)} %bitcast.121), calls=%async_computation.8 | async-start | bytes 4194304
  396.5 61.2 %copy-start.8 = (bf16[4,4,2]{1,2,0:T(2,128)(2,1)S(1)}, bf16[4,4,2]{1,2,0:T(2,128)(2,1)}, u32[]{:S(2)}) copy-start(bf16[4,4,2]{1,2,0:T(2,128)(2,1)} %param.36) | copy-start | bytes 196
  450.4 26.9 %all-to-all-start.1 = ((bf16[16,8,4096]{2,1,0:T(8,128)(2,1)}), bf16[16,8,4096]{2,1,0:T(8,128)(2,1)S(1)}, u32[]{:S(2)}, u32[]{:S(2)}) async-start(bf16[16,8,4096]{2,1,0:T(8,128)(2,1)} %copy.87), calls=%async_computation.2 | async-start | bytes 2097152 | tf_op jit(solution)/shard_map/all_to_all | solution.py:164
Sparse Core Ops, SparseCore 0:
  15.8 85.9 all-reduce.3
  207.3 89.8 all-reduce.5
  319.8 46.7 all-gather.2
  396.7 50.9 reduce-scatter.2
where the time goes:
time: 489 us; the launch traced here: 485 us
  waiting for transfers between devices  293 us (60%)
  local copies, waits for them, and re-layouts  58.7 us (12%)
  blocking collectives  46.9 us (10%)
  matrix products  38.5 us (8%)
  other arithmetic  19.2 us (4%)
  between operations  14.1 us (3%)
  starting transfers between devices  9.47 us (2%)
  loops' own time  5.32 us (1%)
    unnamed x5, waiting for transfers between devices  87.8 us
    psum x1, waiting for transfers between devices, per_device(): lax.psum(projected.astype(jnp.bfloat16), 'exp').astype(jnp.float32)  86 us
    reduce_scatter x1, waiting for transfers between devices, per_device(): lax.psum_scatter(jnp.dot(hidden, w_down[0], preferred_element_type=jnp.fl...  51.1 us
    dynamic_slice x64, local copies, waits for them, and re-layouts, per_device(): final_local, local_out = lax.scan(advance, zero_state, series)  47 us
    all_gather x1, waiting for transfers between devices, per_device(): everything = lax.all_gather(arrived, 'seq', axis=0, tiled=True)  46.7 us
    all_gather x2, blocking collectives, entering(): lax.all_gather(a.astype(kind), axis)  26.2 us
    all_to_all x1, blocking collectives, per_device(): lax.all_to_all(jnp.tile(outgoing, (splits, 1, 1)), 'exp', split_axis=0, c...  20.6 us
    all_to_all x1, waiting for transfers between devices, per_device(): lax.all_to_all(own_rows.astype(jnp.bfloat16), 'exp', split_axis=0, concat...  19.5 us
  transfers between devices with their start and end apart: 6, of which 6 were waited for; matrix products, arithmetic and copies ran while one was open for 1% of the time, Pallas kernels for 0%

commit v1 on v0

--- a/solution.py
+++ b/solution.py
@@ -2,6 +2,7 @@
 import jax.numpy as jnp
 from jax import lax
 from jax.sharding import PartitionSpec as P
+from jax.lax import all_to_all, axis_size
 
 D = 4096
 STATE = 16
@@ -147,7 +148,15 @@
     arrived = lax.all_to_all(
         jnp.tile(outgoing, (splits, 1, 1)), "exp", split_axis=0, concat_axis=0, tiled=True
     )
-    everything = lax.all_gather(arrived, "seq", axis=0, tiled=True)
+    everything = jnp.concatenate(
+        all_to_all(
+            jnp.stack([arrived for _ in range(axis_size("seq"))]),
+            axis_name="seq",
+            split_axis=0,
+            concat_axis=0,
+        ),
+        axis=0,
+    )
     row_block = everything
     expert_row_block = row_block.reshape(-1, D)
     gate_act = jnp.dot(expert_row_block, w_gate[0], preferred_element_type=jnp.float32)

time: 489 us -> 574 us (1.17)
  blocking collectives: 46.9 us -> 146 us
  waiting for transfers between devices: 293 us -> 243 us
  local copies, waits for them, and re-layouts: 58.7 us -> 101 us
    all_to_all x0 -> x1, blocking collectives: none -> 99.4 us  [per_device(): all_to_all(jnp.stack([arrived for _ in range(axis_size('seq'))]), axis_na...]
    mul x128, local copies, waits for them, and re-layouts: 0.74 us -> 88.1 us  [advance(): (step_now * value_now)[:, None, :] * input_now[:, :, None]]
    all_gather x1 -> x0, waiting for transfers between devices: 46.7 us -> none  [per_device(): everything = lax.all_gather(arrived, 'seq', axis=0, tiled=True)]
    dynamic_slice x64, local copies, waits for them, and re-layouts: 47 us -> 0.88 us  [per_device(): final_local, local_out = lax.scan(advance, zero_state, series)]
    unnamed x5 -> x4, waiting for transfers between devices: 87.8 us -> 87.8 us
  transfers between devices with their start and end apart: 6 -> 5, of which waited for: 6 -> 5; matrix products, arithmetic and copies ran while one was open for 1% -> 0% of each run, Pallas kernels for 0% -> 0%
where the time goes in v1:
time: 574 us; the launch traced here: 571 us
  waiting for transfers between devices  243 us (42%)
  blocking collectives  146 us (25%)
  local copies, waits for them, and re-layouts  101 us (18%)
  matrix products  34.6 us (6%)
  other arithmetic  18.2 us (3%)
  between operations  14.2 us (2%)
  starting transfers between devices  9.26 us (2%)
    all_to_all x1, blocking collectives, per_device(): all_to_all(jnp.stack([arrived for _ in range(axis_size('seq'))]), axis_na...  99.4 us
    mul x128, local copies, waits for them, and re-layouts, advance(): (step_now * value_now)[:, None, :] * input_now[:, :, None]  88.1 us
    unnamed x4, waiting for transfers between devices  87.8 us
    psum x1, waiting for transfers between devices, per_device(): lax.psum(projected.astype(jnp.bfloat16), 'exp').astype(jnp.float32)  86 us
    reduce_scatter x1, waiting for transfers between devices, per_device(): lax.psum_scatter(jnp.dot(hidden, w_down[0], preferred_element_type=jnp.fl...  47.1 us
    all_gather x2, blocking collectives, entering(): lax.all_gather(a.astype(kind), axis)  26.2 us
    all_to_all x1, blocking collectives, per_device(): lax.all_to_all(jnp.tile(outgoing, (splits, 1, 1)), 'exp', split_axis=0, c...  20.5 us
    all_to_all x1, waiting for transfers between devices, per_device(): lax.all_to_all(own_rows.astype(jnp.bfloat16), 'exp', split_axis=0, concat...  19.5 us
  transfers between devices with their start and end apart: 5, of which 5 were waited for; matrix products, arithmetic and copies ran while one was open for 0% of the time, Pallas kernels for 0%

profile of v1, /device:TPU:2, one launch (start us, length us, event | category | flops | bytes accessed | tf_op | source)
XLA Modules:
  0.0 570.8 jit_solution(6527493295630914067)
XLA Ops:
  6.6 0.8 slice.38
  7.4 1.9 collective-permute-start
  9.3 0.9 fusion.37
  10.2 2.2 collective-permute-done
  12.4 1.1 maximum_convert_fusion
  13.5 1.2 fusion.33
  14.7 1.0 convolution_convert_fusion.3
  15.7 86.0 %all-reduce.4.cloned.1.call-done = bf16[64,4,288]{2,0,1:T(8,128)(2,1)} async-done(((bf16[64,4,288]{2,0,1:T(8,128)(2,1)}), bf16[64,4,288]{2,0,1:T(8,128)(2,1)}) %all-reduce.4.cloned.1.call-update) | async-done | bytes 147472 | tf_op jit(solution)/shard_map/psum | solution.py:103
  101.8 1.2 fusion.29
  103.6 1.0 fusion.36
  104.7 0.7 copy.75
  105.4 52.9 %while.37 = (s32[]{:T(128)}, f32[4,16,512]{2,1,0:T(8,128)S(1)}, f32[64,4,512]{2,1,0:T(4,128)S(1)}, f32[16,512]{1,0:T(8,128)S(1)}, f32[64,4,512]{2,1,0:T(4,128)S(...) while((s32[]{:T(128)}, f32[4,16,512]{2,1,0:T(8,128)S(1)}, f32[64,4,512]{2,1,0:T(4,128)S(1)}, ...), condition=%wide.region_3.4_spmd.clone, body=%wide.region_2.3_spmd.clone.sunk | while | flops 165891 | bytes 353131 | solution.py:115
  107.1 0.7 dynamic-slice_bitcast_fusion.10
  122.8 0.7 dynamic-slice_bitcast_fusion.10
  138.5 0.7 dynamic-slice_bitcast_fusion.10
  158.3 13.1 %all-gather = bf16[32,16,512]{2,1,0:T(8,128)(2,1)S(1)} all-gather(bf16[4,16,512]{2,1,0:T(8,128)(2,1)S(1)} %convert_element_type.103), channel_id=2, replica_groups=mesh['seq'=8,'exp'=16] {'seq'}, dimensions={0}, use_global_device_ids=true | all-gather | bytes 589824 | tf_op jit(solution)/shard_map/all_gather | solution.py:24
  171.4 13.1 %all_gather.10 = bf16[8,4,16,512]{3,2,1,0:T(8,128)(2,1)S(1)} all-gather(bf16[1,4,16,512]{3,2,1,0:T(8,128)(2,1)S(1)} %exponential_convert_fusion), channel_id=1, replica_groups=mesh['seq'=8,'exp'=16] {'seq'}, dimensions={0}, use_global_device_ids=true | all-gather | bytes 589824 | tf_op jit(solution)/shard_map/all_gather | solution.py:24
  184.7 57.0 %while.36 = (s32[]{:T(128)}, f32[4,16,512]{2,1,0:T(8,128)S(1)}, f32[64,4,512]{2,1,0:T(4,128)S(1)}, f32[64,4,512]{2,1,0:T(4,128)S(1)}, f32[16,512]{1,0:T(8,128)S(...) while((s32[]{:T(128)}, f32[4,16,512]{2,1,0:T(8,128)S(1)}, ...), condition=%wide.region_8.9_spmd, body=%wide.region_6.8_spmd.sunk | while | flops 196610 | bytes 378481 | solution.py:119
  242.2 4.8 convolution_convert_fusion.1
  249.3 87.7 %all-reduce.6.cloned.1.call-done = bf16[64,4,4096]{2,0,1:T(8,128)(2,1)} async-done(((bf16[64,4,4096]{2,0,1:T(8,128)(2,1)}), bf16[64,4,4096]{2,0,1:T(8,128)(2,1)}) %all-reduce.6.cloned.1.call-update) | async-done | bytes 2097168
  337.0 1.0 constant_dynamic-slice_fusion.1
  338.9 20.5 %all_to_all.15 = bf16[16,8,4096]{2,1,0:T(8,128)(2,1)S(1)} all-to-all(bf16[16,8,4096]{2,1,0:T(8,128)(2,1)S(1)} %bitcast.109), channel_id=1, replica_groups=mesh['seq'=8,'exp'=16] {'exp'}, dimensions={0} | all-to-all | bytes 2097152 | tf_op jit(solution)/shard_map/all_to_all | solution.py:148
  359.5 1.0 stack.2
  360.5 99.4 %all_to_all.16 = bf16[8,16,8,4096]{3,2,1,0:T(8,128)(2,1)S(1)} all-to-all(bf16[8,16,8,4096]{3,2,1,0:T(8,128)(2,1)S(1)} %stack.2), channel_id=1, replica_groups=mesh['seq'=8,'exp'=16] {'seq'}, dimensions={0} | all-to-all | bytes 16777216 | tf_op jit(solution)/shard_map/all_to_all | solution.py:152
  459.9 8.3 %fusion.2 = f32[1024,768]{1,0:T(8,128)} fusion(bf16[1024,4096]{1,0:T(8,128)(2,1)S(1)} %bitcast.106, bf16[1,4096,768]{2,1,0:T(8,128)(2,1)S(1)} %bitcast.118), kind=kOutput, calls=%fused_computation.16 | convolution fusion | flops 6442450944 | bytes 17825792 | tf_op jit(solution)/shard_map/dot_general | solution.py:163
  468.2 8.8 %fusion.12 = bf16[128,8,768]{2,1,0:T(8,128)(2,1)S(1)} fusion(f32[1024,768]{1,0:T(8,128)} %fusion.2, bf16[1024,4096]{1,0:T(8,128)(2,1)S(1)} %bitcast.107, bf16[1,4096,768]{2,1,0:T(8,128)(2,1)S(1)} %bitcast.120), kind=kOutput, calls=%fused_computation.29 | convolution fusion | flops 6447169536 | bytes 19398656 | tf_op jit(solution)/shard_map/dot_general | solution.py:162
  477.0 8.9 %convolution_convert_fusion = bf16[128,8,4096]{2,0,1:T(8,128)(2,1)} fusion(bf16[1,768,4096]{2,1,0:T(8,128)(2,1)S(1)} %bitcast.122, bf16[128,8,768]{2,1,0:T(8,128)(2,1)S(1)} %fusion.12), kind=kOutput, calls=%fused_computation.14 | convolution fusion | flops 6446645248 | bytes 16252928 | tf_op jit(solution)/shard_map/dot_general | solution.py:166
  486.0 47.1 %reduce-scatter.3.cloned.1.call-done = bf16[16,8,4096]{2,0,1:T(8,128)(2,1)} async-done(((bf16[128,8,4096]{2,0,1:T(8,128)(2,1)}), bf16[16,8,4096]{2,0,1:T(8,128)(2,1)}) %reduce-scatter.3.cloned.1.call-update) | async-done | bytes 1048592 | tf_op jit(solution)/shard_map/reduce_scatter | solution.py:165
  533.0 2.8 copy.87
  535.8 7.2 %all-to-all-start.2 = ((bf16[16,8,4096]{2,1,0:T(8,128)(2,1)}), bf16[16,8,4096]{2,1,0:T(8,128)(2,1)S(1)}, u32[]{:S(2)}, u32[]{:S(2)}) async-start(bf16[16,8,4096]{2,1,0:T(8,128)(2,1)} %copy.87), calls=%async_computation.3 | async-start | bytes 2097152 | tf_op jit(solution)/shard_map/all_to_all | solution.py:173
  543.2 19.5 %all-to-all-done.2 = bf16[16,8,4096]{2,1,0:T(8,128)(2,1)S(1)} async-done(((bf16[16,8,4096]{2,1,0:T(8,128)(2,1)}), bf16[16,8,4096]{2,1,0:T(8,128)(2,1)S(1)}, u32[]{:S(2)}, u32[]{:S(2)}) %all-to-all-start.2) | async-done | bytes 1048608 | tf_op jit(solution)/shard_map/all_to_all | solution.py:173
  562.9 1.4 fusion.7
  (717 shorter events, 107.3 us)
Async XLA Ops:
  6.5 8.1 %copy-start = (bf16[512,288]{0,1:T(8,128)(2,1)S(1)}, bf16[512,288]{0,1:T(8,128)(2,1)}, u32[]{:S(2)}) copy-start(bf16[512,288]{0,1:T(8,128)(2,1)} %param.27) | copy-start | bytes 884740
  6.5 9.2 %copy-start.5 = (f32[16,512]{1,0:T(8,128)S(1)}, f32[16,512]{1,0:T(8,128)}, u32[]{:S(2)}) copy-start(f32[16,512]{1,0:T(8,128)} %param.30) | copy-start | bytes 98308
  6.5 95.2 %copy-start.4 = (bf16[256,512]{1,0:T(8,128)(2,1)S(1)}, bf16[256,512]{1,0:T(8,128)(2,1)}, u32[]{:S(2)}) copy-start(bf16[256,512]{1,0:T(8,128)(2,1)} %param.28) | copy-start | bytes 786436
  6.5 95.2 %copy-start.8 = (f32[512]{0:T(512)S(1)}, f32[512]{0:T(512)}, u32[]{:S(2)}) copy-start(f32[512]{0:T(512)} %param.29) | copy-start | bytes 6148
  6.5 95.2 %all-reduce.4.cloned.1.call-start = ((), (), s32[]{:S(2)}) async-start(), calls=%async_computation.4 | async-start | bytes 393216 | tf_op jit(solution)/shard_map/psum | solution.py:103
  7.4 5.0 collective-permute-start
  15.7 321.3 %all-reduce.6.cloned.1.call-start = ((), (), s32[]{:S(2)}) async-start(), calls=%async_computation.6 | async-start | bytes 4194304
  104.6 137.1 %copy-start.3 = (bf16[64,4,512]{2,1,0:T(4,128)(2,1)S(1)}, bf16[64,4,512]{2,1,0:T(4,128)(2,1)}, u32[]{:S(2)}) copy-start(bf16[64,4,512]{2,1,0:T(4,128)(2,1)} %param.24) | copy-start | bytes 786436
  104.7 137.1 %copy-start.9 = (f32[512]{0:T(512)S(1)}, f32[512]{0:T(512)}, u32[]{:S(2)}) copy-start(f32[512]{0:T(512)} %param.31) | copy-start | bytes 6148
  242.2 4.9 copy-start.7
  242.2 5.7 %copy-start.11 = (u32[128]{0:T(128)S(1)}, u32[128]{0:T(128)}, u32[]{:S(2)}) copy-start(u32[128]{0:T(128)} %constant.77) | copy-start | bytes 1540
  242.2 95.8 %copy-start.2 = (bf16[4,4,4096]{2,1,0:T(4,128)(2,1)S(1)}, bf16[4,4,4096]{2,1,0:T(4,128)(2,1)}, u32[]{:S(2)}) copy-start(bf16[4,4,4096]{2,1,0:T(4,128)(2,1)} %param.33) | copy-start | bytes 393220
  242.2 96.1 %copy-start.6 = (f32[4096]{0:T(1024)S(1)}, f32[4096]{0:T(1024)}, u32[]{:S(2)}) copy-start(f32[4096]{0:T(1024)} %param.34) | copy-start | bytes 49156
  247.1 286.0 %reduce-scatter.3.cloned.1.call-start = ((), (), s32[]{:S(2)}) async-start(), calls=%async_computation.5 | async-start | bytes 9437184 | tf_op jit(solution)/shard_map/reduce_scatter | solution.py:165
  359.5 100.4 %slice-start = ((s8[6291456]{0:T(1024)(128)(4,1)}), s8[2097152]{0:T(1024)(128)(4,1)S(1)}, s32[]{:S(2)}) async-start(s8[6291456]{0:T(1024)(128)(4,1)} %bitcast.117), calls=%async_computation.7 | async-start | bytes 4194304
  360.5 99.4 %slice-start.1 = ((s8[6291456]{0:T(1024)(128)(4,1)}), s8[4194304]{0:T(1024)(128)(4,1)S(1)}, s32[]{:S(2)}) async-start(s8[6291456]{0:T(1024)(128)(4,1)} %bitcast.117), calls=%async_computation.8 | async-start | bytes 8388608
  360.5 107.7 %slice-start.2 = ((s8[6291456]{0:T(1024)(128)(4,1)}), s8[4194304]{0:T(1024)(128)(4,1)S(1)}, s32[]{:S(2)}) async-start(s8[6291456]{0:T(1024)(128)(4,1)} %bitcast.119), calls=%async_computation.9 | async-start | bytes 8388608
  459.9 8.3 %slice-start.3 = ((s8[6291456]{0:T(1024)(128)(4,1)}), s8[2097152]{0:T(1024)(128)(4,1)S(1)}, s32[]{:S(2)}) async-start(s8[6291456]{0:T(1024)(128)(4,1)} %bitcast.119), calls=%async_computation.10 | async-start | bytes 4194304
  459.9 17.1 %slice-start.4 = ((s8[6291456]{0:T(1024)(128)(4,1)}), s8[4194304]{0:T(1024)(128)(4,1)S(1)}, s32[]{:S(2)}) async-start(s8[6291456]{0:T(1024)(128)(4,1)} %bitcast.121), calls=%async_computation.11 | async-start | bytes 8388608
  468.2 8.8 %slice-start.5 = ((s8[6291456]{0:T(1024)(128)(4,1)}), s8[2097152]{0:T(1024)(128)(4,1)S(1)}, s32[]{:S(2)}) async-start(s8[6291456]{0:T(1024)(128)(4,1)} %bitcast.121), calls=%async_computation.12 | async-start | bytes 4194304
  485.9 57.1 %copy-start.10 = (bf16[4,4,2]{1,2,0:T(2,128)(2,1)S(1)}, bf16[4,4,2]{1,2,0:T(2,128)(2,1)}, u32[]{:S(2)}) copy-start(bf16[4,4,2]{1,2,0:T(2,128)(2,1)} %param.36) | copy-start | bytes 196
  486.0 78.3 %copy-start.1 = (bf16[512,288]{0,1:T(8,128)(2,1)S(1)}, bf16[512,288]{0,1:T(8,128)(2,1)}, u32[]{:S(2)}) copy-start(bf16[512,288]{0,1:T(8,128)(2,1)} %param.27) | copy-start | bytes 884740
  535.8 26.9 %all-to-all-start.2 = ((bf16[16,8,4096]{2,1,0:T(8,128)(2,1)}), bf16[16,8,4096]{2,1,0:T(8,128)(2,1)S(1)}, u32[]{:S(2)}, u32[]{:S(2)}) async-start(bf16[16,8,4096]{2,1,0:T(8,128)(2,1)} %copy.87), calls=%async_computation.3 | async-start | bytes 2097152 | tf_op jit(solution)/shard_map/all_to_all | solution.py:173
Sparse Core Ops, SparseCore 0:
  15.8 85.9 all-reduce.3
  247.2 89.7 all-reduce.5
  486.1 46.9 reduce-scatter.2
